TPU v7x, 128 devices: a whole 4x4x4 slice. The times are simulated.
128 devices in a mesh: tx: 32 (over y, x, core), ty: 4 (over z).
Axes of the slice: x: 4, y: 4, z: 4, core: 2. Of those that a mesh axis runs over, the one named last changes fastest.
Arguments:
- points: bfloat16 [524288, 128], P(('tx', 'ty')), may hold values from -6 to 6
- embed_weight: bfloat16 [128, 512], replicated, may hold values from -0.5 to 0.5
- inner_weights: bfloat16 [1, 512, 512], replicated, may hold values from -0.25 to 0.25
- output_weight: bfloat16 [512, 128], replicated, may hold values from -0.25 to 0.25
- counts: int32 [128, 512], replicated, may hold values from 1 to 16, as said below
- point_order: int32 [128, 4096], P(('tx', 'ty')), may hold values from 0 to 4095, each once within a row
- inducing: bfloat16 [128, 128], replicated, may hold values from -6 to 6
- first_proj: bfloat16 [4, 128, 128], replicated, may hold values from -0.5 to 0.5
- second_proj: bfloat16 [4, 128, 128], replicated, may hold values from -0.5 to 0.5
- mixing: bfloat16 [8, 128, 128], replicated, may hold values from -0.1875 to 0.1875
Outputs:
- encoded: bfloat16 [524288, 128], P(('tx', 'ty'))
Inputs may be any that keep to these rules, and one draw needn't show every extreme that they name: Row s sums to 4096. For every source s and every device, the counts of s in the 4 tiles that device holds sum to exactly 32, and one of those 4 entries equals 16. Row s is a permutation of the local points of source s: the points of tile g are point_order[s, offsets[s, g] + c] for c below counts[s, g].
All inputs are finite; a program needn't handle non-finite values.
Results may differ from a plain program's by a relative error of at most 0.025.
Values may be sent and summed in bfloat16 or wider, within the bound.
A program may use at most 64 MiB of HBM per device.

v0:
```python
import math
import jax
import jax.numpy as jnp
from jax import lax
from jax.sharding import PartitionSpec as P

HEADS = 2
TLX = 2
TLY = 2
sharpness = 32.0
epsilon = 1e-06
neighbour_steps = ((-1, -1), (-1, 0), (-1, 1), (0, -1), (0, 1), (1, -1), (1, 0), (1, 1))


def padded_2(block, sides, width):
    for axis, dim in sides:
        count = lax.axis_size(axis)
        forward = [(i, i + 1) for i in range(count - 1)]
        backward = [(target, source) for source, target in forward]
        low = lax.ppermute(
            lax.slice_in_dim(block, block.shape[dim] - width, None, axis=dim), axis, forward
        )
        high = lax.ppermute(lax.slice_in_dim(block, 0, width, axis=dim), axis, backward)
        block = jnp.concatenate([low, block, high], axis=dim)
    return block


def unit_heads(projected, head_count):
    pieces = projected.reshape(
        projected.shape[:-1] + (head_count, projected.shape[-1] // head_count)
    )
    magnitude = jnp.sqrt(jnp.sum(pieces * pieces, axis=-1, keepdims=True) + epsilon)
    return (pieces / magnitude).reshape(projected.shape).astype(jnp.bfloat16)


def attend(query_rows, key_rows, value_rows, weight_mask):
    head_width = query_rows.shape[-1] // HEADS
    outputs = []
    for head_id in range(HEADS):
        lower = head_id * head_width
        upper = lower + head_width
        scores = jnp.dot(
            query_rows[:, lower:upper],
            key_rows[:, lower:upper].T,
            preferred_element_type=jnp.float32,
        )
        weights = jnp.exp(sharpness * scores) * weight_mask[None, :]
        totals = jnp.sum(weights, axis=1, keepdims=True)
        numer = jnp.dot(
            weights.astype(jnp.bfloat16),
            value_rows[:, lower:upper],
            preferred_element_type=jnp.float32,
        )
        outputs.append(numer / totals)
    return jnp.concatenate(outputs, axis=1).astype(jnp.bfloat16)


def block_layout(tallies, quota):
    before = jnp.cumsum(tallies, axis=0) - tallies
    through = (before + tallies).T
    slot_ids = jnp.arange(quota, dtype=jnp.int32)
    which = jnp.sum((slot_ids[None, :, None] >= through[:, None, :]).astype(jnp.int32), axis=2)
    base = jnp.take_along_axis(before.T, which, axis=1)
    return (before, which, slot_ids[None, :] - base)


def local_rows(index, source_rows, block):
    column_ids = jnp.arange(source_rows.shape[0], dtype=jnp.int32)

    def pick_block(index_block):
        table = (index_block[:, None] == column_ids[None, :]).astype(jnp.bfloat16)
        return jnp.dot(table, source_rows, preferred_element_type=jnp.float32).astype(jnp.bfloat16)

    picked = lax.map(pick_block, index.reshape(-1, block))
    return picked.reshape(index.shape[0], source_rows.shape[1])


def place_rows(index, rows, total, block):
    target_ids = jnp.arange(total, dtype=jnp.int32).reshape(-1, block)

    def place_block(target_block):
        table = (target_block[:, None] == index[None, :]).astype(jnp.bfloat16)
        return jnp.dot(table, rows, preferred_element_type=jnp.float32).astype(jnp.bfloat16)

    placed = lax.map(place_block, target_ids)
    return placed.reshape(total, rows.shape[1])


def slot_table(tallies, before, capacity, quota):
    slot_ids = jnp.arange(capacity, dtype=jnp.int32)
    packed_ids = jnp.arange(quota, dtype=jnp.int32)
    starts = before.T
    live = slot_ids[None, None, :] < tallies.T[:, :, None]
    hits = (
        packed_ids[None, None, None, :] == starts[:, :, None, None] + slot_ids[None, None, :, None]
    )
    return (hits & live[..., None]).astype(jnp.bfloat16)


def expand(blocks, table):
    return jnp.einsum("otcq,oqe->toce", table, blocks, preferred_element_type=jnp.float32).astype(
        jnp.bfloat16
    )


def collapse(slots, table):
    return jnp.einsum("otcq,toce->oqe", table, slots, preferred_element_type=jnp.float32).astype(
        jnp.bfloat16
    )


def body(
    points,
    embed_weight,
    inner_weights,
    output_weight,
    counts,
    point_order,
    inducing,
    first_proj,
    second_proj,
    mixing,
):
    along_x = lax.axis_size("tx")
    along_y = lax.axis_size("ty")
    devices = along_x * along_y
    index_x = lax.axis_index("tx")
    index_y = lax.axis_index("ty")
    own_index = index_x * along_y + index_y
    point_count = points.shape[0]
    capacity = 2 * point_count // counts.shape[1]
    per_device = TLX * TLY
    width = output_weight.shape[1]
    tile_rows = devices * capacity
    quota = point_count // devices
    block = math.gcd(512, point_count)
    hidden = jax.nn.silu(jnp.dot(points, embed_weight, preferred_element_type=jnp.float32)).astype(
        jnp.bfloat16
    )
    hidden = jax.nn.silu(
        jnp.dot(hidden, inner_weights[0], preferred_element_type=jnp.float32)
    ).astype(jnp.bfloat16)
    features = jnp.dot(hidden, output_weight, preferred_element_type=jnp.float32).astype(
        jnp.bfloat16
    )
    own_counts = lax.dynamic_index_in_dim(counts, own_index, 0, keepdims=False)
    own_offsets = jnp.cumsum(own_counts) - own_counts

    def by_owner(table):
        return (
            table.reshape(along_x, TLX, along_y, TLY)
            .transpose(1, 3, 0, 2)
            .reshape(per_device, devices)
        )

    slot_ids = jnp.arange(capacity, dtype=jnp.int32)
    send_counts = by_owner(own_counts)
    send_starts = by_owner(own_offsets)
    inbound = counts.reshape(devices, along_x, TLX, along_y, TLY)
    inbound = lax.dynamic_index_in_dim(inbound, index_x, 1, keepdims=False)
    inbound = lax.dynamic_index_in_dim(inbound, index_y, 2, keepdims=False)
    inbound = inbound.transpose(1, 2, 0).reshape(per_device, devices)
    live_slots = slot_ids[None, None, :] < inbound[:, :, None]
    key_mask = live_slots.astype(jnp.float32).reshape(per_device, tile_rows)
    send_before, send_which, send_within = block_layout(send_counts, quota)
    packed_pos = jnp.take_along_axis(send_starts.T, send_which, axis=1) + send_within
    packed_index = point_order[0][packed_pos].reshape(-1)
    packed = local_rows(packed_index, features, block).reshape(devices, quota, width)
    send_table = slot_table(send_counts, send_before, capacity, quota)
    outgoing = expand(packed, send_table)
    arrived = lax.all_to_all(outgoing, ("tx", "ty"), split_axis=1, concat_axis=1, tiled=True)
    arrived = arrived.reshape(per_device, tile_rows, width)
    all_rows = arrived.reshape(per_device * tile_rows, width)
    first_keys = unit_heads(
        jnp.dot(all_rows, first_proj[1], preferred_element_type=jnp.float32), HEADS
    ).reshape(per_device, tile_rows, width)
    first_values = (
        jnp.dot(all_rows, first_proj[2], preferred_element_type=jnp.float32)
        .astype(jnp.bfloat16)
        .reshape(per_device, tile_rows, width)
    )
    inducing_queries = unit_heads(
        jnp.dot(inducing, first_proj[0], preferred_element_type=jnp.float32), HEADS
    )
    first_attended = jax.vmap(attend, in_axes=(None, 0, 0, 0))(
        inducing_queries, first_keys, first_values, key_mask
    )
    summary = (
        inducing.astype(jnp.float32)[None]
        + jnp.einsum(
            "tic,ce->tie", first_attended, first_proj[3], preferred_element_type=jnp.float32
        )
    ).astype(jnp.bfloat16)
    tile_grid = summary.reshape(TLX, TLY, summary.shape[1], width)
    padded = padded_2(tile_grid, (("tx", 0), ("ty", 1)), 1)
    stacked = jnp.stack(
        [
            padded[1 + steps[0] : 1 + steps[0] + TLX, 1 + steps[1] : 1 + steps[1] + TLY]
            for steps in neighbour_steps
        ]
    )
    mixture = tile_grid.astype(jnp.float32) + jnp.einsum(
        "dxyic,dce->xyie", stacked, mixing, preferred_element_type=jnp.float32
    )
    mixture = mixture.astype(jnp.bfloat16).reshape(per_device * summary.shape[1], width)
    point_queries = unit_heads(
        jnp.dot(all_rows, second_proj[0], preferred_element_type=jnp.float32), HEADS
    ).reshape(per_device, tile_rows, width)
    second_keys = unit_heads(
        jnp.dot(mixture, second_proj[1], preferred_element_type=jnp.float32), HEADS
    ).reshape(per_device, -1, width)
    second_values = (
        jnp.dot(mixture, second_proj[2], preferred_element_type=jnp.float32)
        .astype(jnp.bfloat16)
        .reshape(per_device, -1, width)
    )
    every_key = jnp.ones((second_keys.shape[1],), jnp.float32)
    second_attended = jax.vmap(attend, in_axes=(0, 0, 0, None))(
        point_queries, second_keys, second_values, every_key
    )
    result = (
        arrived.astype(jnp.float32)
        + jnp.einsum(
            "trc,ce->tre", second_attended, second_proj[3], preferred_element_type=jnp.float32
        )
    ).astype(jnp.bfloat16)
    result_slots = result.reshape(per_device, devices, capacity, width)
    coming = lax.all_to_all(result_slots, ("tx", "ty"), split_axis=1, concat_axis=1, tiled=True)
    returned = collapse(coming, send_table)
    return place_rows(packed_index, returned.reshape(point_count, width), point_count, block)


def solution(mesh):
    placed = (P(("tx", "ty"), None), P(), P(), P(), P(), P(("tx", "ty"), None), P(), P(), P(), P())
    return jax.shard_map(
        body, mesh=mesh, in_specs=placed, out_specs=P(("tx", "ty"), None), check_vma=False
    )
```

profile of v0, /device:TPU:1, one launch (start us, length us, event | category | flops | bytes accessed | tf_op | source)
XLA Modules:
  0.0 279.4 jit_solution(15943603343116851955)
XLA Ops:
  5.2 26.7 %gather_fusion.2 = s32[4096]{0:T(1024)S(1)} fusion(s32[128,4]{1,0:T(8,128)S(1)} %subtract_bitcast_fusion.1, s32[4096]{0:T(1024)S(1)} %reshape.218), kind=kCustom, calls=%fused_computation.1.clone | custom fusion | bytes 65536 | tf_op jit(solution)/shard_map/jit(take_along_axis)/gather | solution.py:63
  31.9 33.1 %gather_fusion.1 = s32[4096]{0:T(1024)S(1)} fusion(s32[128,4]{0,1:T(4,128)S(1)} %bitcast.236, s32[4096]{0:T(1024)S(1)} %reshape.218), kind=kCustom, calls=%fused_computation.clone | custom fusion | bytes 65536 | tf_op jit(solution)/shard_map/jit(take_along_axis)/gather | solution.py:166
  65.8 23.0 %gather_fusion = s32[4096]{0:T(1024)S(1)} fusion(s32[4096]{0:T(1024)S(1)} %bitcast.237, s32[4096]{0:T(1024)S(1)} %broadcast_clamp_fusion), kind=kCustom, calls=%fused_computation.2 | custom fusion | bytes 49152 | tf_op jit(solution)/shard_map/gather | solution.py:167
  88.9 6.4 %fusion.21 = f32[4096,512]{1,0:T(8,128)} fusion(bf16[4096,128]{1,0:T(8,128)(2,1)S(1)} %copy-done, bf16[128,512]{1,0:T(8,128)(2,1)S(1)} %copy-done.18, bf16[1,512,512]{2,1,0:T(8,128)(2,1)S(1)} %copy-done.17), kind=kOutput, calls=%fused_computation.38 | convolution fusion | flops 2694840320 | bytes 10092544 | tf_op jit(solution)/shard_map/dot_general | solution.py:141
  95.3 5.7 %convolution_convert_fusion.1 = bf16[4096,128]{1,0:T(8,128)(2,1)S(1)} fusion(bf16[512,128]{1,0:T(8,128)(2,1)S(1)} %copy-done.19, f32[4096,512]{1,0:T(8,128)} %fusion.21), kind=kOutput, calls=%fused_computation.22 | convolution fusion | flops 547880960 | bytes 9568256 | tf_op jit(solution)/shard_map/dot_general | solution.py:143
  101.1 12.9 %while.22 = (s32[]{:T(128)}, bf16[8,512,128]{2,1,0:T(8,128)(2,1)S(1)}, s32[8,512]{1,0:T(8,128)S(1)}, bf16[4096,128]{1,0:T(8,128)(2,1)S(1)}, s32[]{:T(128)}) while((s32[]{:T(128)}, bf16[8,512,128]{2,1,0:T(8,128)(2,1)S(1)}, s32[8,512]{1,0:T(8,128)S(1)}, bf16[4096,128]{1,0:T(8,128)(2,1)S(1)}, s32[]{:T(128)}) %tuple.56), condition=%wide.region_5.7_spmd.clone, body=%wide.region_4.6_spmd.clone.sunk | while | flops 539033600 | bytes 1185861 | solution.py:74
  114.4 5.1 %convert_bitcast_fusion = bf16[4,128,16,128]{3,2,0,1:T(8,128)(2,1)} fusion(bf16[128,32,128,1]{2,1,3,0:T(8,128)(2,1)S(1)} %bitcast.252, s32[128,4,16]{2,1,0:T(4,128)S(1)} %iota_add_fusion, pred[128,4,16]{2,1,0:T(4,128)(4,1)S(1)} %iota_compare_fusion.9), kind=kOutput, calls=%fused_computation.65 | convolution fusion | flops 68681728 | bytes 3186688 | tf_op jit(solution)/shard_map/otcq,oqe->toce/dot_general | solution.py:101
  119.5 12.0 %all-to-all-start = ((bf16[4,128,16,128]{3,2,0,1:T(8,128)(2,1)}), bf16[4,128,16,128]{3,2,0,1:T(8,128)(2,1)}, u32[]{:S(2)}, u32[]{:S(2)}) async-start(bf16[4,128,16,128]{3,2,0,1:T(8,128)(2,1)} %convert_bitcast_fusion), calls=%async_computation | async-start | bytes 4194304 | tf_op jit(solution)/shard_map/all_to_all | solution.py:171
  134.1 27.6 %all-to-all-done = bf16[4,128,16,128]{3,2,0,1:T(8,128)(2,1)} async-done(((bf16[4,128,16,128]{3,2,0,1:T(8,128)(2,1)}), bf16[4,128,16,128]{3,2,0,1:T(8,128)(2,1)}, u32[]{:S(2)}, u32[]{:S(2)}) %all-to-all-start) | async-done | bytes 2097184 | tf_op jit(solution)/shard_map/all_to_all | solution.py:171
  166.1 4.5 %convert_element_type.119 = bf16[4,2048,128]{1,0,2:T(4,128)(2,1)} reshape(bf16[8192,2,64]{0,2,1:T(8,128)(2,1)} %divide_convert_fusion) | data formatting | bytes 4194304 | tf_op jit(solution)/shard_map/convert_element_type | solution.py:33
  175.5 2.7 bitcast_reduce_fusion.1
  181.5 2.8 collective-permute-start
  187.6 2.8 convert_element_type.114
  196.8 3.9 %copy.66 = f32[4,128,16,128]{3,2,1,0:T(8,128)} copy(bf16[4,128,16,128]{3,2,0,1:T(8,128)(2,1)} %all-to-all-done) | data formatting | bytes 6291456 | tf_op jit(solution)/shard_map/convert_element_type | solution.py:222
  212.1 8.4 %all-to-all-start.1 = ((bf16[4,128,16,128]{3,2,0,1:T(8,128)(2,1)}), bf16[4,128,16,128]{3,2,0,1:T(8,128)(2,1)S(1)}, u32[]{:S(2)}, u32[]{:S(2)}) async-start(bf16[4,128,16,128]{3,2,0,1:T(8,128)(2,1)} %copy.94), calls=%async_computation.1 | async-start | bytes 4194304 | tf_op jit(solution)/shard_map/all_to_all | solution.py:228
  220.7 30.4 %all-to-all-done.1 = bf16[4,128,16,128]{3,2,0,1:T(8,128)(2,1)S(1)} async-done(((bf16[4,128,16,128]{3,2,0,1:T(8,128)(2,1)}), bf16[4,128,16,128]{3,2,0,1:T(8,128)(2,1)S(1)}, u32[]{:S(2)}, u32[]{:S(2)}) %all-to-all-start.1) | async-done | bytes 2097184 | tf_op jit(solution)/shard_map/all_to_all | solution.py:228
  251.0 5.7 %bitcast_convert_fusion.4 = bf16[128,32,128]{2,1,0:T(8,128)(2,1)} fusion(bf16[4,128,16,128]{3,2,0,1:T(8,128)(2,1)S(1)} %all-to-all-done.1, s32[128,4,16]{2,1,0:T(4,128)S(1)} %iota_add_fusion, pred[128,4,16]{2,1,0:T(4,128)(4,1)S(1)} %copy-done.16), kind=kOutput, calls=%fused_computation.58 | convolution fusion | flops 68157440 | bytes 3186688 | tf_op jit(solution)/shard_map/otcq,toce->oqe/dot_general | solution.py:107
  256.8 20.9 %while.23 = (s32[]{:T(128)}, bf16[8,512,128]{2,1,0:T(8,128)(2,1)S(1)}, s32[8,512]{1,0:T(8,128)S(1)}, s32[128,32]{1,0:T(8,128)}, bf16[4096,128]{1,0:T(8,128)(2,1)}, /*index=5*/s32[4096]{0:T(1024)S(1)}, s32[]{:T(128)}) while((s32[]{:T(128)}, bf16[8,512,128]{2,1,0:T(8,128)(2,1)S(1)}, s32[8,512]{1,0:T(8,128)S(1)}, ...), condition=%wide.wide.region_15.17_spmd, body=%wide.wide.region_14.16_spmd.sunk | while | flops 539033600 | bytes 1202261 | solution.py:85
  256.9 2.6 fusion.151
  259.5 2.6 fusion.151
  262.1 2.6 fusion.151
  264.7 2.6 fusion.151
  267.3 2.6 fusion.151
  275.2 2.6 fusion.151
  (169 shorter events, 62.0 us)
Async XLA Ops:
  0.0 88.8 %copy-start = (bf16[4096,128]{1,0:T(8,128)(2,1)S(1)}, bf16[4096,128]{1,0:T(8,128)(2,1)}, u32[]{:S(2)}) copy-start(bf16[4096,128]{1,0:T(8,128)(2,1)} %param.16) | copy-start | bytes 3145732
  65.8 23.1 %copy-start.17 = (bf16[1,512,512]{2,1,0:T(8,128)(2,1)S(1)}, bf16[1,512,512]{2,1,0:T(8,128)(2,1)}, u32[]{:S(2)}) copy-start(bf16[1,512,512]{2,1,0:T(8,128)(2,1)} %param.18) | copy-start | bytes 1572868
  65.8 23.1 %copy-start.18 = (bf16[128,512]{1,0:T(8,128)(2,1)S(1)}, bf16[128,512]{1,0:T(8,128)(2,1)}, u32[]{:S(2)}) copy-start(bf16[128,512]{1,0:T(8,128)(2,1)} %param.17) | copy-start | bytes 393220
  88.9 6.4 %copy-start.19 = (bf16[512,128]{1,0:T(8,128)(2,1)S(1)}, bf16[512,128]{1,0:T(8,128)(2,1)}, u32[]{:S(2)}) copy-start(bf16[512,128]{1,0:T(8,128)(2,1)} %param.19) | copy-start | bytes 393220
  114.3 5.1 %copy-start.15 = (pred[128,4,16]{2,1,0:T(4,128)(4,1)}, pred[128,4,16]{2,1,0:T(4,128)(4,1)S(1)}, u32[]{:S(2)}) copy-start(pred[128,4,16]{2,1,0:T(4,128)(4,1)S(1)} %iota_compare_fusion.9) | copy-start | bytes 24580
  119.5 12.0 %copy-start.5 = (s32[128,512]{1,0:T(8,128)S(1)}, s32[128,512]{1,0:T(8,128)}, u32[]{:S(2)}) copy-start(s32[128,512]{1,0:T(8,128)} %param.20) | copy-start | bytes 786436
  119.5 12.2 %copy-start.11 = (bf16[4,128,128]{2,1,0:T(8,128)(2,1)S(1)}, bf16[4,128,128]{2,1,0:T(8,128)(2,1)}, u32[]{:S(2)}) copy-start(bf16[4,128,128]{2,1,0:T(8,128)(2,1)} %param.23) | copy-start | bytes 393220
  119.5 12.8 %copy-start.13 = (bf16[128,128]{1,0:T(8,128)(2,1)S(1)}, bf16[128,128]{1,0:T(8,128)(2,1)}, u32[]{:S(2)}) copy-start(bf16[128,128]{1,0:T(8,128)(2,1)} %param.22) | copy-start | bytes 98308
  119.5 12.8 %copy-start.9 = (bf16[4,128,128]{2,1,0:T(8,128)(2,1)S(1)}, bf16[4,128,128]{2,1,0:T(8,128)(2,1)}, u32[]{:S(2)}) copy-start(bf16[4,128,128]{2,1,0:T(8,128)(2,1)} %param.24) | copy-start | bytes 393220
  119.5 42.2 %all-to-all-start = ((bf16[4,128,16,128]{3,2,0,1:T(8,128)(2,1)}), bf16[4,128,16,128]{3,2,0,1:T(8,128)(2,1)}, u32[]{:S(2)}, u32[]{:S(2)}) async-start(bf16[4,128,16,128]{3,2,0,1:T(8,128)(2,1)} %convert_bitcast_fusion), calls=%async_computation | async-start | bytes 4194304 | tf_op jit(solution)/shard_map/all_to_all | solution.py:171
  170.6 2.5 copy-start.12
  173.8 1.7 copy-start.8
  181.5 8.9 %collective-permute-start = (bf16[1,2,128,128]{3,2,1,0:T(8,128)(2,1)S(1)}, bf16[1,2,128,128]{3,2,1,0:T(8,128)(2,1)S(1)}, u32[]{:S(2)}, u32[]{:S(2)}) collective-permute-start(bf16[1,2,128,128]{3,2,1,0:T(8,128)(2,1)S(1)} %get-tuple-element.106), channel_id=1, source_target_pairs={{0,4},{4,8},{8,12},{12,16},{16,20},{20,24},{24,28},{28,32},{32,36}... | collective-permute-start | bytes 196616 | tf_op jit(solution)/shard_map/ppermute | solution.py:20
  184.3 6.1 %collective-permute-start.1 = (bf16[1,2,128,128]{3,2,1,0:T(8,128)(2,1)S(1)}, bf16[1,2,128,128]{3,2,1,0:T(8,128)(2,1)S(1)}, u32[]{:S(2)}, u32[]{:S(2)}) collective-permute-start(bf16[1,2,128,128]{3,2,1,0:T(8,128)(2,1)S(1)} %get-tuple-element.107), channel_id=1, source_target_pairs={{4,0},{8,4},{12,8},{16,12},{20,16},{24,20},{28,24},{32,28},{36,32}... | collective-permute-start | bytes 196616 | tf_op jit(solution)/shard_map/ppermute | solution.py:23
  190.5 10.3 %collective-permute-start.2 = (bf16[4,1,128,128]{3,2,1,0:T(8,128)(2,1)S(1)}, bf16[4,1,128,128]{3,2,1,0:T(8,128)(2,1)S(1)}, u32[]{:S(2)}, u32[]{:S(2)}) collective-permute-start(bf16[4,1,128,128]{3,2,1,0:T(8,128)(2,1)S(1)} %get-tuple-element.101), channel_id=1, source_target_pairs={{0,1},{1,2},{2,3},{4,5},{5,6},{6,7},{8,9},{9,10},{10,11},{12,13},{... | collective-permute-start | bytes 393224 | tf_op jit(solution)/shard_map/ppermute | solution.py:20
  192.9 7.8 %collective-permute-start.3 = (bf16[4,1,128,128]{3,2,1,0:T(8,128)(2,1)S(1)}, bf16[4,1,128,128]{3,2,1,0:T(8,128)(2,1)S(1)}, u32[]{:S(2)}, u32[]{:S(2)}) collective-permute-start(bf16[4,1,128,128]{3,2,1,0:T(8,128)(2,1)S(1)} %get-tuple-element.100), channel_id=1, source_target_pairs={{1,0},{2,1},{3,2},{5,4},{6,5},{7,6},{9,8},{10,9},{11,10},{13,12},{... | collective-permute-start | bytes 393224 | tf_op jit(solution)/shard_map/ppermute | solution.py:23
  196.8 4.2 %copy-start.7 = (bf16[8,128,128]{2,1,0:T(8,128)(2,1)S(1)}, bf16[8,128,128]{2,1,0:T(8,128)(2,1)}, u32[]{:S(2)}) copy-start(bf16[8,128,128]{2,1,0:T(8,128)(2,1)} %param.25) | copy-start | bytes 786436
  196.8 4.7 %copy-start.14 = (bf16[128,128]{1,0:T(8,128)(2,1)S(1)}, bf16[128,128]{1,0:T(8,128)(2,1)}, u32[]{:S(2)}) copy-start(bf16[128,128]{1,0:T(8,128)(2,1)} %copy.85) | copy-start | bytes 98308
  200.8 1.1 copy-start.10
  207.1 2.2 copy-start.3
  210.1 41.0 %copy-start.16 = (pred[128,4,16]{2,1,0:T(4,128)(4,1)S(1)}, pred[128,4,16]{2,1,0:T(4,128)(4,1)}, u32[]{:S(2)}) copy-start(pred[128,4,16]{2,1,0:T(4,128)(4,1)} %copy-done.15) | copy-start | bytes 24580
  212.1 39.0 %all-to-all-start.1 = ((bf16[4,128,16,128]{3,2,0,1:T(8,128)(2,1)}), bf16[4,128,16,128]{3,2,0,1:T(8,128)(2,1)S(1)}, u32[]{:S(2)}, u32[]{:S(2)}) async-start(bf16[4,128,16,128]{3,2,0,1:T(8,128)(2,1)} %copy.94), calls=%async_computation.1 | async-start | bytes 4194304 | tf_op jit(solution)/shard_map/all_to_all | solution.py:228
  220.6 36.1 %copy-start.6 = (s32[128,32]{1,0:T(8,128)}, s32[128,32]{1,0:T(8,128)S(1)}, u32[]{:S(2)}) copy-start(s32[128,32]{1,0:T(8,128)S(1)} %reshape.197) | copy-start | bytes 49156
  277.8 1.6 copy-start.1
  (2 other events, 1.7 us)
where the time goes:
time: 280 us; the launch traced here: 279 us
  local copies, waits for them, and re-layouts  113 us (40%)
  matrix products  73.6 us (26%)
  waiting for transfers between devices  58 us (21%)
  starting transfers between devices  29.1 us (10%)
  other arithmetic  4.16 us (1%)
    gather x5, local copies, waits for them, and re-layouts, body(): jnp.take_along_axis(send_starts.T, send_which, axis=1) + send_within  33.4 us
    all_to_all x1, waiting for transfers between devices, body(): lax.all_to_all(result_slots, ('tx', 'ty'), split_axis=1, concat_axis=1, t...  30.4 us
    all_to_all x1, waiting for transfers between devices, body(): lax.all_to_all(outgoing, ('tx', 'ty'), split_axis=1, concat_axis=1, tiled...  27.6 us
    gather x3, local copies, waits for them, and re-layouts, block_layout(): base = jnp.take_along_axis(before.T, which, axis=1)  26.9 us
    gather x2, local copies, waits for them, and re-layouts, body(): packed_index = point_order[0][packed_pos].reshape(-1)  23.1 us
    dot_general x8, matrix products, place_block(): jnp.dot(table, rows, preferred_element_type=jnp.float32)  20.7 us
    dot_general x8, matrix products, pick_block(): jnp.dot(table, source_rows, preferred_element_type=jnp.float32)  12.7 us
    all_to_all x1, starting transfers between devices, body(): lax.all_to_all(outgoing, ('tx', 'ty'), split_axis=1, concat_axis=1, tiled...  12 us
  transfers between devices with their start and end apart: 6, of which 2 were waited for; matrix products, arithmetic and copies ran while one was open for 5% of the time, Pallas kernels for 0%

commit v1 on v0

--- a/solution.py
+++ b/solution.py
@@ -3,6 +3,7 @@
 import jax.numpy as jnp
 from jax import lax
 from jax.sharding import PartitionSpec as P
+from jax.lax import all_to_all, axis_size
 
 HEADS = 2
 TLX = 2
@@ -225,7 +226,16 @@
         )
     ).astype(jnp.bfloat16)
     result_slots = result.reshape(per_device, devices, capacity, width)
-    coming = lax.all_to_all(result_slots, ("tx", "ty"), split_axis=1, concat_axis=1, tiled=True)
+    post_desk = lambda payload, which_dim, dim_k: jnp.concatenate(
+        all_to_all(
+            jnp.stack(jnp.split(payload, axis_size(("tx", "ty")), axis=which_dim)),
+            ("tx", "ty"),
+            0,
+            0,
+        ),
+        axis=dim_k,
+    )
+    coming = post_desk(result_slots, 1, 1)
     returned = collapse(coming, send_table)
     return place_rows(packed_index, returned.reshape(point_count, width), point_count, block)
 

time: 280 us -> 356 us (1.27)
  local copies, waits for them, and re-layouts: 113 us -> 189 us
    unnamed x46 -> x173, local copies, waits for them, and re-layouts: 3.35 us -> 80.3 us
  transfers between devices with their start and end apart: 6 -> 6, of which waited for: 2 -> 2; matrix products, arithmetic and copies ran while one was open for 5% -> 4% of each run, Pallas kernels for 0% -> 0%
where the time goes in v1:
time: 356 us; the launch traced here: 355 us
  local copies, waits for them, and re-layouts  189 us (53%)
  matrix products  73.6 us (21%)
  waiting for transfers between devices  58 us (16%)
  starting transfers between devices  29.1 us (8%)
  other arithmetic  4.16 us (1%)
    unnamed x173, local copies, waits for them, and re-layouts  80.3 us
    gather x5, local copies, waits for them, and re-layouts, body(): jnp.take_along_axis(send_starts.T, send_which, axis=1) + send_within  33.4 us
    all_to_all x1, waiting for transfers between devices, body(): all_to_all(jnp.stack(jnp.split(payload, axis_size(('tx', 'ty')), axis=whi...  30.4 us
    all_to_all x1, waiting for transfers between devices, body(): lax.all_to_all(outgoing, ('tx', 'ty'), split_axis=1, concat_axis=1, tiled...  27.6 us
    gather x3, local copies, waits for them, and re-layouts, block_layout(): base = jnp.take_along_axis(before.T, which, axis=1)  26.9 us
    gather x2, local copies, waits for them, and re-layouts, body(): packed_index = point_order[0][packed_pos].reshape(-1)  23.1 us
    dot_general x8, matrix products, place_block(): jnp.dot(table, rows, preferred_element_type=jnp.float32)  20.7 us
    dot_general x8, matrix products, pick_block(): jnp.dot(table, source_rows, preferred_element_type=jnp.float32)  12.7 us
  transfers between devices with their start and end apart: 6, of which 2 were waited for; matrix products, arithmetic and copies ran while one was open for 4% of the time, Pallas kernels for 0%

profile of v1, /device:TPU:1, one launch (start us, length us, event | category | flops | bytes accessed | tf_op | source)
XLA Modules:
  0.0 355.0 jit_solution(17868853047802596054)
XLA Ops:
  5.2 26.7 %gather_fusion.2 = s32[4096]{0:T(1024)S(1)} fusion(s32[128,4]{1,0:T(8,128)S(1)} %subtract_bitcast_fusion.1, s32[4096]{0:T(1024)S(1)} %reshape.226), kind=kCustom, calls=%fused_computation.1.clone | custom fusion | bytes 65536 | tf_op jit(solution)/shard_map/jit(take_along_axis)/gather | solution.py:64
  31.9 33.1 %gather_fusion.1 = s32[4096]{0:T(1024)S(1)} fusion(s32[128,4]{0,1:T(4,128)S(1)} %bitcast.1012, s32[4096]{0:T(1024)S(1)} %reshape.226), kind=kCustom, calls=%fused_computation.clone | custom fusion | bytes 65536 | tf_op jit(solution)/shard_map/jit(take_along_axis)/gather | solution.py:167
  65.8 23.0 %gather_fusion = s32[4096]{0:T(1024)S(1)} fusion(s32[4096]{0:T(1024)S(1)} %bitcast.1013, s32[4096]{0:T(1024)S(1)} %broadcast_clamp_fusion), kind=kCustom, calls=%fused_computation.2 | custom fusion | bytes 49152 | tf_op jit(solution)/shard_map/gather | solution.py:168
  88.9 6.4 %fusion.21 = f32[4096,512]{1,0:T(8,128)} fusion(bf16[4096,128]{1,0:T(8,128)(2,1)S(1)} %copy-done, bf16[128,512]{1,0:T(8,128)(2,1)S(1)} %copy-done.18, bf16[1,512,512]{2,1,0:T(8,128)(2,1)S(1)} %copy-done.17), kind=kOutput, calls=%fused_computation.38 | convolution fusion | flops 2694840320 | bytes 10092544 | tf_op jit(solution)/shard_map/dot_general | solution.py:142
  95.3 5.7 %convolution_convert_fusion.1 = bf16[4096,128]{1,0:T(8,128)(2,1)S(1)} fusion(bf16[512,128]{1,0:T(8,128)(2,1)S(1)} %copy-done.19, f32[4096,512]{1,0:T(8,128)} %fusion.21), kind=kOutput, calls=%fused_computation.22 | convolution fusion | flops 547880960 | bytes 9568256 | tf_op jit(solution)/shard_map/dot_general | solution.py:144
  101.1 12.9 %while.22 = (s32[]{:T(128)}, bf16[8,512,128]{2,1,0:T(8,128)(2,1)S(1)}, s32[8,512]{1,0:T(8,128)S(1)}, bf16[4096,128]{1,0:T(8,128)(2,1)S(1)}, s32[]{:T(128)}) while((s32[]{:T(128)}, bf16[8,512,128]{2,1,0:T(8,128)(2,1)S(1)}, s32[8,512]{1,0:T(8,128)S(1)}, bf16[4096,128]{1,0:T(8,128)(2,1)S(1)}, s32[]{:T(128)}) %tuple.56), condition=%wide.region_5.7_spmd.clone, body=%wide.region_4.6_spmd.clone.sunk | while | flops 539033600 | bytes 1185861 | solution.py:75
  114.4 5.1 %convert_bitcast_fusion = bf16[4,128,16,128]{3,2,0,1:T(8,128)(2,1)} fusion(bf16[128,32,128,1]{2,1,3,0:T(8,128)(2,1)S(1)} %bitcast.1155, s32[128,4,16]{2,1,0:T(4,128)S(1)} %iota_add_fusion, pred[128,4,16]{2,1,0:T(4,128)(4,1)S(1)} %iota_compare_fusion.9), kind=kOutput, calls=%fused_computation.66 | convolution fusion | flops 68681728 | bytes 3186688 | tf_op jit(solution)/shard_map/otcq,oqe->toce/dot_general | solution.py:102
  119.5 12.0 %all-to-all-start = ((bf16[4,128,16,128]{3,2,0,1:T(8,128)(2,1)}), bf16[4,128,16,128]{3,2,0,1:T(8,128)(2,1)}, u32[]{:S(2)}, u32[]{:S(2)}) async-start(bf16[4,128,16,128]{3,2,0,1:T(8,128)(2,1)} %convert_bitcast_fusion), calls=%async_computation | async-start | bytes 4194304 | tf_op jit(solution)/shard_map/all_to_all | solution.py:172
  134.1 27.6 %all-to-all-done = bf16[4,128,16,128]{3,2,0,1:T(8,128)(2,1)} async-done(((bf16[4,128,16,128]{3,2,0,1:T(8,128)(2,1)}), bf16[4,128,16,128]{3,2,0,1:T(8,128)(2,1)}, u32[]{:S(2)}, u32[]{:S(2)}) %all-to-all-start) | async-done | bytes 2097184 | tf_op jit(solution)/shard_map/all_to_all | solution.py:172
  166.1 4.5 %convert_element_type.119 = bf16[4,2048,128]{1,0,2:T(4,128)(2,1)} reshape(bf16[8192,2,64]{0,2,1:T(8,128)(2,1)} %divide_convert_fusion) | data formatting | bytes 4194304 | tf_op jit(solution)/shard_map/convert_element_type | solution.py:34
  175.5 2.7 bitcast_reduce_fusion.1
  181.5 2.8 collective-permute-start
  187.6 2.8 convert_element_type.114
  196.8 3.9 %copy.482 = f32[4,128,16,128]{3,2,1,0:T(8,128)} copy(bf16[4,128,16,128]{3,2,0,1:T(8,128)(2,1)} %all-to-all-done) | data formatting | bytes 6291456 | tf_op jit(solution)/shard_map/convert_element_type | solution.py:223
  287.7 8.4 %all-to-all-start.1 = ((bf16[128,4,1,16,128]{4,3,1,2,0:T(8,128)(2,1)}), bf16[128,4,1,16,128]{4,3,1,2,0:T(8,128)(2,1)S(1)}, u32[]{:S(2)}, u32[]{:S(2)}) async-start(bf16[128,4,1,16,128]{4,3,1,2,0:T(8,128)(2,1)} %constant_dynamic-update-slice_fusion.8), calls=%async_computation.1 | async-start | bytes 4194304 | tf_op jit(solution)/shard_map/all_to_all | solution.py:230
  296.3 30.4 %all-to-all-done.1 = bf16[128,4,1,16,128]{4,3,1,2,0:T(8,128)(2,1)S(1)} async-done(((bf16[128,4,1,16,128]{4,3,1,2,0:T(8,128)(2,1)}), bf16[128,4,1,16,128]{4,3,1,2,0:T(8,128)(2,1)S(1)}, u32[]{:S(2)}, u32[]{:S(2)}) %all-to-all-start.1) | async-done | bytes 2097184 | tf_op jit(solution)/shard_map/all_to_all | solution.py:230
  326.7 5.7 %bitcast_convert_fusion.4 = bf16[128,32,128]{2,1,0:T(8,128)(2,1)} fusion(bf16[128,4,1,16,128]{4,3,1,2,0:T(8,128)(2,1)S(1)} %all-to-all-done.1, s32[128,4,16]{2,1,0:T(4,128)S(1)} %iota_add_fusion, pred[128,4,16]{2,1,0:T(4,128)(4,1)S(1)} %copy-done.16), kind=kOutput, calls=%fused_computation.59 | convolution fusion | flops 68157440 | bytes 3186688 | tf_op jit(solution)/shard_map/otcq,toce->oqe/dot_general | solution.py:108
  332.5 20.9 %while.23 = (s32[]{:T(128)}, bf16[8,512,128]{2,1,0:T(8,128)(2,1)S(1)}, s32[8,512]{1,0:T(8,128)S(1)}, s32[128,32]{1,0:T(8,128)}, bf16[4096,128]{1,0:T(8,128)(2,1)}, /*index=5*/s32[4096]{0:T(1024)S(1)}, s32[]{:T(128)}) while((s32[]{:T(128)}, bf16[8,512,128]{2,1,0:T(8,128)(2,1)S(1)}, s32[8,512]{1,0:T(8,128)S(1)}, ...), condition=%wide.wide.region_15.17_spmd, body=%wide.wide.region_14.16_spmd.sunk | while | flops 539033600 | bytes 1202261 | solution.py:86
  335.1 2.6 fusion.145
  337.7 2.6 fusion.145
  340.3 2.6 fusion.145
  342.9 2.6 fusion.145
  345.6 2.6 fusion.145
  348.2 2.6 fusion.145
  (296 shorter events, 137.6 us)
Async XLA Ops:
  0.0 88.8 %copy-start = (bf16[4096,128]{1,0:T(8,128)(2,1)S(1)}, bf16[4096,128]{1,0:T(8,128)(2,1)}, u32[]{:S(2)}) copy-start(bf16[4096,128]{1,0:T(8,128)(2,1)} %param.16) | copy-start | bytes 3145732
  65.8 23.1 %copy-start.17 = (bf16[1,512,512]{2,1,0:T(8,128)(2,1)S(1)}, bf16[1,512,512]{2,1,0:T(8,128)(2,1)}, u32[]{:S(2)}) copy-start(bf16[1,512,512]{2,1,0:T(8,128)(2,1)} %param.18) | copy-start | bytes 1572868
  65.8 23.1 %copy-start.18 = (bf16[128,512]{1,0:T(8,128)(2,1)S(1)}, bf16[128,512]{1,0:T(8,128)(2,1)}, u32[]{:S(2)}) copy-start(bf16[128,512]{1,0:T(8,128)(2,1)} %param.17) | copy-start | bytes 393220
  88.9 6.4 %copy-start.19 = (bf16[512,128]{1,0:T(8,128)(2,1)S(1)}, bf16[512,128]{1,0:T(8,128)(2,1)}, u32[]{:S(2)}) copy-start(bf16[512,128]{1,0:T(8,128)(2,1)} %param.19) | copy-start | bytes 393220
  114.3 5.1 %copy-start.15 = (pred[128,4,16]{2,1,0:T(4,128)(4,1)}, pred[128,4,16]{2,1,0:T(4,128)(4,1)S(1)}, u32[]{:S(2)}) copy-start(pred[128,4,16]{2,1,0:T(4,128)(4,1)S(1)} %iota_compare_fusion.9) | copy-start | bytes 24580
  119.5 12.0 %copy-start.5 = (s32[128,512]{1,0:T(8,128)S(1)}, s32[128,512]{1,0:T(8,128)}, u32[]{:S(2)}) copy-start(s32[128,512]{1,0:T(8,128)} %param.20) | copy-start | bytes 786436
  119.5 12.2 %copy-start.11 = (bf16[4,128,128]{2,1,0:T(8,128)(2,1)S(1)}, bf16[4,128,128]{2,1,0:T(8,128)(2,1)}, u32[]{:S(2)}) copy-start(bf16[4,128,128]{2,1,0:T(8,128)(2,1)} %param.23) | copy-start | bytes 393220
  119.5 12.8 %copy-start.13 = (bf16[128,128]{1,0:T(8,128)(2,1)S(1)}, bf16[128,128]{1,0:T(8,128)(2,1)}, u32[]{:S(2)}) copy-start(bf16[128,128]{1,0:T(8,128)(2,1)} %param.22) | copy-start | bytes 98308
  119.5 12.8 %copy-start.9 = (bf16[4,128,128]{2,1,0:T(8,128)(2,1)S(1)}, bf16[4,128,128]{2,1,0:T(8,128)(2,1)}, u32[]{:S(2)}) copy-start(bf16[4,128,128]{2,1,0:T(8,128)(2,1)} %param.24) | copy-start | bytes 393220
  119.5 42.2 %all-to-all-start = ((bf16[4,128,16,128]{3,2,0,1:T(8,128)(2,1)}), bf16[4,128,16,128]{3,2,0,1:T(8,128)(2,1)}, u32[]{:S(2)}, u32[]{:S(2)}) async-start(bf16[4,128,16,128]{3,2,0,1:T(8,128)(2,1)} %convert_bitcast_fusion), calls=%async_computation | async-start | bytes 4194304 | tf_op jit(solution)/shard_map/all_to_all | solution.py:172
  170.6 2.5 copy-start.12
  173.8 1.7 copy-start.8
  181.5 8.9 %collective-permute-start = (bf16[1,2,128,128]{3,2,1,0:T(8,128)(2,1)S(1)}, bf16[1,2,128,128]{3,2,1,0:T(8,128)(2,1)S(1)}, u32[]{:S(2)}, u32[]{:S(2)}) collective-permute-start(bf16[1,2,128,128]{3,2,1,0:T(8,128)(2,1)S(1)} %get-tuple-element.106), channel_id=1, source_target_pairs={{0,4},{4,8},{8,12},{12,16},{16,20},{20,24},{24,28},{28,32},{32,36}... | collective-permute-start | bytes 196616 | tf_op jit(solution)/shard_map/ppermute | solution.py:21
  184.3 6.1 %collective-permute-start.1 = (bf16[1,2,128,128]{3,2,1,0:T(8,128)(2,1)S(1)}, bf16[1,2,128,128]{3,2,1,0:T(8,128)(2,1)S(1)}, u32[]{:S(2)}, u32[]{:S(2)}) collective-permute-start(bf16[1,2,128,128]{3,2,1,0:T(8,128)(2,1)S(1)} %get-tuple-element.107), channel_id=1, source_target_pairs={{4,0},{8,4},{12,8},{16,12},{20,16},{24,20},{28,24},{32,28},{36,32}... | collective-permute-start | bytes 196616 | tf_op jit(solution)/shard_map/ppermute | solution.py:24
  190.5 10.2 %collective-permute-start.2 = (bf16[4,1,128,128]{3,2,1,0:T(8,128)(2,1)S(1)}, bf16[4,1,128,128]{3,2,1,0:T(8,128)(2,1)S(1)}, u32[]{:S(2)}, u32[]{:S(2)}) collective-permute-start(bf16[4,1,128,128]{3,2,1,0:T(8,128)(2,1)S(1)} %get-tuple-element.101), channel_id=1, source_target_pairs={{0,1},{1,2},{2,3},{4,5},{5,6},{6,7},{8,9},{9,10},{10,11},{12,13},{... | collective-permute-start | bytes 393224 | tf_op jit(solution)/shard_map/ppermute | solution.py:21
  192.9 7.8 %collective-permute-start.3 = (bf16[4,1,128,128]{3,2,1,0:T(8,128)(2,1)S(1)}, bf16[4,1,128,128]{3,2,1,0:T(8,128)(2,1)S(1)}, u32[]{:S(2)}, u32[]{:S(2)}) collective-permute-start(bf16[4,1,128,128]{3,2,1,0:T(8,128)(2,1)S(1)} %get-tuple-element.100), channel_id=1, source_target_pairs={{1,0},{2,1},{3,2},{5,4},{6,5},{7,6},{9,8},{10,9},{11,10},{13,12},{... | collective-permute-start | bytes 393224 | tf_op jit(solution)/shard_map/ppermute | solution.py:24
  200.8 1.3 copy-start.14
  200.9 1.6 copy-start.10
  207.6 2.2 copy-start.3
  287.7 39.0 %copy-start.16 = (pred[128,4,16]{2,1,0:T(4,128)(4,1)S(1)}, pred[128,4,16]{2,1,0:T(4,128)(4,1)}, u32[]{:S(2)}) copy-start(pred[128,4,16]{2,1,0:T(4,128)(4,1)} %copy-done.15) | copy-start | bytes 24580
  287.7 39.0 %all-to-all-start.1 = ((bf16[128,4,1,16,128]{4,3,1,2,0:T(8,128)(2,1)}), bf16[128,4,1,16,128]{4,3,1,2,0:T(8,128)(2,1)S(1)}, u32[]{:S(2)}, u32[]{:S(2)}) async-start(bf16[128,4,1,16,128]{4,3,1,2,0:T(8,128)(2,1)} %constant_dynamic-update-slice_fusion.8), calls=%async_computation.1 | async-start | bytes 4194304 | tf_op jit(solution)/shard_map/all_to_all | solution.py:230
  296.2 36.1 %copy-start.6 = (s32[128,32]{1,0:T(8,128)}, s32[128,32]{1,0:T(8,128)S(1)}, u32[]{:S(2)}) copy-start(s32[128,32]{1,0:T(8,128)S(1)} %reshape.205) | copy-start | bytes 49156
  353.4 1.0 copy-start.4
  353.4 1.6 copy-start.1
  (2 other events, 1.7 us)
